TPU v7x, 32 devices: a whole 2x2x4 slice. The times are simulated.
32 devices in a mesh: gen: 4 (over y, x), fit: 8 (over z, core).
Axes of the slice: x: 2, y: 2, z: 4, core: 2. Of those that a mesh axis runs over, the one named last changes fastest.
Arguments:
- raw_columns: bfloat16 [8, 2000, 2000], P(None, 'gen', 'fit'), as said below
- pivot_pairs: int32 [8], replicated, may hold values from 0 to 3999999, as said below
- collocation: bfloat16 [2000, 4096], P('gen', 'fit'), may hold values from -0.125 to 0.125
- metric_factor: float32 [4096, 4096], P('fit', 'gen'), as said below
Outputs:
- panel: float32 [8, 4096], P('gen', 'fit')
Inputs may be any that keep to these rules, and one draw needn't show every extreme that they name: `pivot_pairs`: 8 distinct orbital-pair indices p * 2000 + q. The entries at the pivots, raw_columns[P, pivot_pairs[Q] // 2000, pivot_pairs[Q] % 2000], form a symmetric positive definite matrix. `metric_factor`: lower triangular with a positive diagonal.
All inputs are finite; a program needn't handle non-finite values.
Results may differ from a plain program's by a relative error of at most 0.0029.
Values may be sent and summed in bfloat16 or wider, within the bound.
No kernel may reach another device: no remote copies, remote signals or barrier semaphores. Data moves between devices by JAX's collectives and lax.ppermute only.
A program may use at most 64 MiB of HBM per device.

v0:
```python
import math
import jax
import jax.numpy as jnp
from jax import lax
from jax.sharding import PartitionSpec as P

NORB = 2000


def spread(value, axis, source):
    kept = jnp.where(lax.axis_index(axis) == source, value, 0).astype(value.dtype)
    return lax.psum(kept, axis)


def project_block(vectors, stacked, orbital_count):
    point_count = stacked.shape[1]
    block_width = math.gcd(point_count, 512)
    block_count = point_count // block_width
    pair_count = stacked.shape[0] - orbital_count
    orbital_part = (
        stacked[:orbital_count].reshape(orbital_count, block_count, block_width).transpose(1, 0, 2)
    )
    pair_part = (
        stacked[orbital_count:].reshape(pair_count, block_count, block_width).transpose(1, 0, 2)
    )

    def one_block(pieces):
        mixed_terms = jnp.einsum(
            "apq,pn->aqn", vectors, pieces[0], preferred_element_type=jnp.float32
        )
        return jnp.sum(mixed_terms * pieces[1].astype(jnp.float32)[None], axis=1)

    blocks = lax.map(one_block, (orbital_part, pair_part))
    return blocks.transpose(1, 0, 2).reshape(vectors.shape[0], point_count)


def on_device(raw_columns, pivot_pairs, collocation, metric_factor):
    vec_total, orb_block, pair_block = raw_columns.shape
    gen_count = lax.axis_size("gen")
    fit_count = lax.axis_size("fit")
    gen_index = lax.axis_index("gen")
    fit_index = lax.axis_index("fit")
    point_dev = metric_factor.shape[0]
    vec_dev = vec_total // gen_count
    pair_first = pivot_pairs // NORB
    pair_second = pivot_pairs % NORB
    row_hits = (
        pair_first[:, None] == gen_index * orb_block + jnp.arange(orb_block)[None, :]
    ).astype(jnp.bfloat16)
    col_hits = (
        pair_second[:, None] == fit_index * pair_block + jnp.arange(pair_block)[None, :]
    ).astype(jnp.float32)
    picked = jnp.einsum("apq,bp->abq", raw_columns, row_hits, preferred_element_type=jnp.float32)
    own_entries = jnp.sum(picked * col_hits[None], axis=2)
    pivot_block = lax.psum(own_entries, ("gen", "fit"))
    factor = jnp.linalg.cholesky(pivot_block)
    flat_columns = raw_columns.reshape(vec_total, orb_block * pair_block).astype(jnp.float32)
    vectors = jax.scipy.linalg.solve_triangular(factor, flat_columns, lower=True)
    vectors = vectors.astype(jnp.bfloat16).reshape(vec_total, orb_block, pair_block)
    group_ratio = fit_count // gen_count
    owner_index = fit_index // group_ratio
    portion = fit_index % group_ratio
    orbital_side = lax.all_gather(collocation, "fit", axis=1, tiled=True)
    wide_slice = lax.dynamic_slice_in_dim(orbital_side, portion * pair_block, pair_block, 0)
    pair_side = spread(wide_slice, "gen", owner_index)
    partial_panel = project_block(
        vectors, jnp.concatenate([orbital_side, pair_side], axis=0), orb_block
    )
    arranged = partial_panel.reshape(gen_count, vec_dev, fit_count, point_dev).transpose(0, 2, 1, 3)
    arranged = arranged.reshape(gen_count * fit_count * vec_dev, point_dev)
    summed = lax.psum_scatter(arranged, ("gen", "fit"), scatter_dimension=0, tiled=True)
    remaining_start = jnp.zeros((vec_total, point_dev), jnp.float32)
    remaining_start = lax.dynamic_update_slice_in_dim(
        remaining_start, summed, gen_index * vec_dev, 0
    )

    def advance(turn_index, carried):
        remaining, solved = carried
        turn_owner = turn_index // group_ratio
        local_start = turn_index % group_ratio * point_dev
        whole_rest = lax.psum(remaining, "gen")
        column_part = lax.dynamic_slice_in_dim(metric_factor, local_start, point_dev, 1)
        candidate = jax.scipy.linalg.solve_triangular(column_part, whole_rest.T, lower=True).T
        holder = jnp.logical_and(fit_index == turn_index, gen_index == turn_owner)
        candidate = jnp.where(holder, candidate, 0.0)
        arrived = spread(candidate, ("gen", "fit"), turn_owner * fit_count + turn_index)
        update = jnp.dot(arrived, column_part.T, precision=lax.Precision.HIGHEST)
        remaining = remaining - jnp.where(gen_index == turn_owner, update, 0.0)
        own_rows = lax.dynamic_slice_in_dim(arrived, gen_index * vec_dev, vec_dev, 0)
        solved = jnp.where(fit_index == turn_index, own_rows, solved)
        return (remaining, solved)

    initial = jnp.zeros((vec_dev, point_dev), jnp.float32)
    remaining, solved = lax.fori_loop(0, fit_count, advance, (remaining_start, initial))
    return solved


def solution(mesh):
    in_specs = (P(None, "gen", "fit"), P(), P("gen", "fit"), P("fit", "gen"))
    out_specs = P("gen", "fit")
    return jax.shard_map(
        on_device, mesh=mesh, in_specs=in_specs, out_specs=out_specs, check_vma=False
    )
```

profile of v0, /device:TPU:0, one launch (start us, length us, event | category | flops | bytes accessed | tf_op | source)
XLA Modules:
  0.0 1175.4 jit_solution(14042528507513244858)
XLA Ops:
  7.3 50.9 %all-gather.2.cloned.1.call-done = bf16[500,4096]{1,0:T(8,128)(2,1)} async-done(((bf16[500,512]{1,0:T(8,128)(2,1)}), bf16[500,4096]{1,0:T(8,128)(2,1)}) %all-gather.2.cloned.1.call-update) | async-done | bytes 4096016 | tf_op jit(solution)/shard_map/all_gather | solution.py:63
  67.0 39.1 %psum.42 = f32[8,8]{0,1:T(8,128)S(1)} all-reduce(f32[8,8]{0,1:T(8,128)S(1)} %bitcast.108), channel_id=1, replica_groups=mesh['gen'=4,'fit'=8] {'gen','fit'}, use_global_device_ids=true, to_apply=%region_2.3 | all-reduce | flops 64 | bytes 512 | tf_op jit(solution)/shard_map/psum | solution.py:55
  108.8 7.2 reshape.130
  116.0 4.1 reshape.104
  123.1 4.2 reshape.132
  127.3 6.0 reshape.105
  133.3 6.5 copy.18
  139.8 6.5 copy.25
  146.3 35.0 %while.31 = (s32[]{:T(128)}, f32[8,8,512]{2,1,0:T(8,128)S(1)}, bf16[8,500,512]{2,1,0:T(8,128)(2,1)}, bf16[8,500,250]{2,1,0:T(8,128)(2,1)}, bf16[8,250,512]{1,2,0:T(8,128)(2,1)}, /*index=5*/s32[]{:T(128)}) while((s32[]{:T(128)}, f32[8,8,512]{2,1,0:T(8,128)S(1)}, bf16[8,500,512]{2,1,0:T(8,128)(2,1)}, bf16[8,500,250]{2,1,0:T(8,128)(2,1)}, ...), condition=%wide.region_7.8_spmd, body=%wide.region_5.7_spmd.sunk | while | flops 1026171904 | bytes 4934221 | solution.py:33
  156.3 3.1 fusion.70
  160.7 3.1 fusion.70
  165.0 3.1 fusion.70
  169.4 3.1 fusion.70
  178.1 3.1 fusion.70
  182.1 122.3 %all-reduce.6.cloned.1.call-done = f32[64,512]{1,0:T(8,128)} async-done(((f32[64,512]{1,0:T(8,128)}), f32[64,512]{1,0:T(8,128)}) %all-reduce.6.cloned.1.call-update) | async-done | bytes 131088
  305.2 863.1 %while.33 = (s32[]{:T(128)}, f32[8,512]{1,0:T(8,128)S(1)}, f32[2,512]{1,0:T(2,128)S(1)}, s32[]{:T(128)}, s32[]{:T(128)}, /*index=5*/f32[512,1024]{1,0:T(8,128)S(...) while((s32[]{:T(128)}, f32[8,512]{1,0:T(8,128)S(1)}, ...), condition=%wide.region_12.13_spmd.clone, body=%wide.region_9.12_spmd.clone.sunk | while | flops 41468964 | bytes 4176043 | solution.py:94
  305.6 10.0 while.34
  315.6 40.1 %custom-call.26 = f32[4,128,128]{1,2,0:T(8,128)S(1)} custom-call(f32[4,128,128]{2,1,0:T(8,128)} %get-tuple-element.386), custom_call_target="InvertDiagBlocksLowerTriangular" | custom-call | tf_op jit(solution)/shard_map/while/body/eval_jaxpr/jit(_solve_triangular)/triangular_solve | solution.py:83
  355.7 15.9 %psum.48 = f32[512,8]{0,1:T(8,128)S(1)} all-reduce(f32[512,8]{0,1:T(8,128)S(1)} %bitcast.105), channel_id=1, replica_groups=mesh['gen'=4,'fit'=8] {'gen'}, use_global_device_ids=true, to_apply=%region_10.10 | all-reduce | flops 4096 | bytes 32768 | tf_op jit(solution)/shard_map/while/body/eval_jaxpr/psum | solution.py:81
  373.1 38.4 %psum.49 = f32[8,512]{1,0:T(8,128)S(1)} all-reduce(f32[8,512]{1,0:T(8,128)S(1)} %fusion.88), channel_id=1, replica_groups=mesh['gen'=4,'fit'=8] {'gen','fit'}, use_global_device_ids=true, to_apply=%region_11.11 | all-reduce | flops 4096 | bytes 32768 | tf_op jit(solution)/shard_map/while/body/eval_jaxpr/psum | solution.py:12
  412.7 10.0 while.34
  422.8 40.1 %custom-call.26 = f32[4,128,128]{1,2,0:T(8,128)S(1)} custom-call(f32[4,128,128]{2,1,0:T(8,128)} %get-tuple-element.386), custom_call_target="InvertDiagBlocksLowerTriangular" | custom-call | tf_op jit(solution)/shard_map/while/body/eval_jaxpr/jit(_solve_triangular)/triangular_solve | solution.py:83
  462.9 16.7 %psum.48 = f32[512,8]{0,1:T(8,128)S(1)} all-reduce(f32[512,8]{0,1:T(8,128)S(1)} %bitcast.105), channel_id=1, replica_groups=mesh['gen'=4,'fit'=8] {'gen'}, use_global_device_ids=true, to_apply=%region_10.10 | all-reduce | flops 4096 | bytes 32768 | tf_op jit(solution)/shard_map/while/body/eval_jaxpr/psum | solution.py:81
  481.1 38.4 %psum.49 = f32[8,512]{1,0:T(8,128)S(1)} all-reduce(f32[8,512]{1,0:T(8,128)S(1)} %fusion.88), channel_id=1, replica_groups=mesh['gen'=4,'fit'=8] {'gen','fit'}, use_global_device_ids=true, to_apply=%region_11.11 | all-reduce | flops 4096 | bytes 32768 | tf_op jit(solution)/shard_map/while/body/eval_jaxpr/psum | solution.py:12
  520.7 10.0 while.34
  530.7 40.1 %custom-call.26 = f32[4,128,128]{1,2,0:T(8,128)S(1)} custom-call(f32[4,128,128]{2,1,0:T(8,128)} %get-tuple-element.386), custom_call_target="InvertDiagBlocksLowerTriangular" | custom-call | tf_op jit(solution)/shard_map/while/body/eval_jaxpr/jit(_solve_triangular)/triangular_solve | solution.py:83
  570.9 16.7 %psum.48 = f32[512,8]{0,1:T(8,128)S(1)} all-reduce(f32[512,8]{0,1:T(8,128)S(1)} %bitcast.105), channel_id=1, replica_groups=mesh['gen'=4,'fit'=8] {'gen'}, use_global_device_ids=true, to_apply=%region_10.10 | all-reduce | flops 4096 | bytes 32768 | tf_op jit(solution)/shard_map/while/body/eval_jaxpr/psum | solution.py:81
  589.1 38.4 %psum.49 = f32[8,512]{1,0:T(8,128)S(1)} all-reduce(f32[8,512]{1,0:T(8,128)S(1)} %fusion.88), channel_id=1, replica_groups=mesh['gen'=4,'fit'=8] {'gen','fit'}, use_global_device_ids=true, to_apply=%region_11.11 | all-reduce | flops 4096 | bytes 32768 | tf_op jit(solution)/shard_map/while/body/eval_jaxpr/psum | solution.py:12
  628.7 10.0 while.34
  638.7 40.1 %custom-call.26 = f32[4,128,128]{1,2,0:T(8,128)S(1)} custom-call(f32[4,128,128]{2,1,0:T(8,128)} %get-tuple-element.386), custom_call_target="InvertDiagBlocksLowerTriangular" | custom-call | tf_op jit(solution)/shard_map/while/body/eval_jaxpr/jit(_solve_triangular)/triangular_solve | solution.py:83
  678.8 16.7 %psum.48 = f32[512,8]{0,1:T(8,128)S(1)} all-reduce(f32[512,8]{0,1:T(8,128)S(1)} %bitcast.105), channel_id=1, replica_groups=mesh['gen'=4,'fit'=8] {'gen'}, use_global_device_ids=true, to_apply=%region_10.10 | all-reduce | flops 4096 | bytes 32768 | tf_op jit(solution)/shard_map/while/body/eval_jaxpr/psum | solution.py:81
  697.0 38.4 %psum.49 = f32[8,512]{1,0:T(8,128)S(1)} all-reduce(f32[8,512]{1,0:T(8,128)S(1)} %fusion.88), channel_id=1, replica_groups=mesh['gen'=4,'fit'=8] {'gen','fit'}, use_global_device_ids=true, to_apply=%region_11.11 | all-reduce | flops 4096 | bytes 32768 | tf_op jit(solution)/shard_map/while/body/eval_jaxpr/psum | solution.py:12
  736.6 10.0 while.34
  746.7 40.1 %custom-call.26 = f32[4,128,128]{1,2,0:T(8,128)S(1)} custom-call(f32[4,128,128]{2,1,0:T(8,128)} %get-tuple-element.386), custom_call_target="InvertDiagBlocksLowerTriangular" | custom-call | tf_op jit(solution)/shard_map/while/body/eval_jaxpr/jit(_solve_triangular)/triangular_solve | solution.py:83
  786.8 16.7 %psum.48 = f32[512,8]{0,1:T(8,128)S(1)} all-reduce(f32[512,8]{0,1:T(8,128)S(1)} %bitcast.105), channel_id=1, replica_groups=mesh['gen'=4,'fit'=8] {'gen'}, use_global_device_ids=true, to_apply=%region_10.10 | all-reduce | flops 4096 | bytes 32768 | tf_op jit(solution)/shard_map/while/body/eval_jaxpr/psum | solution.py:81
  805.0 38.4 %psum.49 = f32[8,512]{1,0:T(8,128)S(1)} all-reduce(f32[8,512]{1,0:T(8,128)S(1)} %fusion.88), channel_id=1, replica_groups=mesh['gen'=4,'fit'=8] {'gen','fit'}, use_global_device_ids=true, to_apply=%region_11.11 | all-reduce | flops 4096 | bytes 32768 | tf_op jit(solution)/shard_map/while/body/eval_jaxpr/psum | solution.py:12
  844.6 10.0 while.34
  854.6 40.1 %custom-call.26 = f32[4,128,128]{1,2,0:T(8,128)S(1)} custom-call(f32[4,128,128]{2,1,0:T(8,128)} %get-tuple-element.386), custom_call_target="InvertDiagBlocksLowerTriangular" | custom-call | tf_op jit(solution)/shard_map/while/body/eval_jaxpr/jit(_solve_triangular)/triangular_solve | solution.py:83
  894.8 16.8 %psum.48 = f32[512,8]{0,1:T(8,128)S(1)} all-reduce(f32[512,8]{0,1:T(8,128)S(1)} %bitcast.105), channel_id=1, replica_groups=mesh['gen'=4,'fit'=8] {'gen'}, use_global_device_ids=true, to_apply=%region_10.10 | all-reduce | flops 4096 | bytes 32768 | tf_op jit(solution)/shard_map/while/body/eval_jaxpr/psum | solution.py:81
  913.0 38.4 %psum.49 = f32[8,512]{1,0:T(8,128)S(1)} all-reduce(f32[8,512]{1,0:T(8,128)S(1)} %fusion.88), channel_id=1, replica_groups=mesh['gen'=4,'fit'=8] {'gen','fit'}, use_global_device_ids=true, to_apply=%region_11.11 | all-reduce | flops 4096 | bytes 32768 | tf_op jit(solution)/shard_map/while/body/eval_jaxpr/psum | solution.py:12
  952.5 10.0 while.34
  962.6 40.1 %custom-call.26 = f32[4,128,128]{1,2,0:T(8,128)S(1)} custom-call(f32[4,128,128]{2,1,0:T(8,128)} %get-tuple-element.386), custom_call_target="InvertDiagBlocksLowerTriangular" | custom-call | tf_op jit(solution)/shard_map/while/body/eval_jaxpr/jit(_solve_triangular)/triangular_solve | solution.py:83
  1002.7 16.8 %psum.48 = f32[512,8]{0,1:T(8,128)S(1)} all-reduce(f32[512,8]{0,1:T(8,128)S(1)} %bitcast.105), channel_id=1, replica_groups=mesh['gen'=4,'fit'=8] {'gen'}, use_global_device_ids=true, to_apply=%region_10.10 | all-reduce | flops 4096 | bytes 32768 | tf_op jit(solution)/shard_map/while/body/eval_jaxpr/psum | solution.py:81
  1020.9 38.4 %psum.49 = f32[8,512]{1,0:T(8,128)S(1)} all-reduce(f32[8,512]{1,0:T(8,128)S(1)} %fusion.88), channel_id=1, replica_groups=mesh['gen'=4,'fit'=8] {'gen','fit'}, use_global_device_ids=true, to_apply=%region_11.11 | all-reduce | flops 4096 | bytes 32768 | tf_op jit(solution)/shard_map/while/body/eval_jaxpr/psum | solution.py:12
  1060.5 10.0 while.34
  1070.6 40.1 %custom-call.26 = f32[4,128,128]{1,2,0:T(8,128)S(1)} custom-call(f32[4,128,128]{2,1,0:T(8,128)} %get-tuple-element.386), custom_call_target="InvertDiagBlocksLowerTriangular" | custom-call | tf_op jit(solution)/shard_map/while/body/eval_jaxpr/jit(_solve_triangular)/triangular_solve | solution.py:83
  1110.7 16.8 %psum.48 = f32[512,8]{0,1:T(8,128)S(1)} all-reduce(f32[512,8]{0,1:T(8,128)S(1)} %bitcast.105), channel_id=1, replica_groups=mesh['gen'=4,'fit'=8] {'gen'}, use_global_device_ids=true, to_apply=%region_10.10 | all-reduce | flops 4096 | bytes 32768 | tf_op jit(solution)/shard_map/while/body/eval_jaxpr/psum | solution.py:81
  1128.9 38.4 %psum.49 = f32[8,512]{1,0:T(8,128)S(1)} all-reduce(f32[8,512]{1,0:T(8,128)S(1)} %fusion.88), channel_id=1, replica_groups=mesh['gen'=4,'fit'=8] {'gen','fit'}, use_global_device_ids=true, to_apply=%region_11.11 | all-reduce | flops 4096 | bytes 32768 | tf_op jit(solution)/shard_map/while/body/eval_jaxpr/psum | solution.py:12
  (282 shorter events, 136.9 us)
Async XLA Ops:
  6.5 51.7 %all-gather.2.cloned.1.call-start = ((), (), s32[]{:S(2)}) async-start(), calls=%async_computation | async-start | bytes 4644864 | tf_op jit(solution)/shard_map/all_gather | solution.py:63
  7.3 139.0 %all-reduce.4.cloned.1.call-start = ((), (), s32[]{:S(2)}) async-start(), calls=%async_computation.1 | async-start | bytes 4194304 | tf_op jit(solution)/shard_map/psum | solution.py:12
  62.9 1.6 copy-start.1
  63.0 3.3 copy-start.3
  63.0 241.5 %all-reduce.6.cloned.1.call-start = ((), (), s32[]{:S(2)}) async-start(), calls=%async_computation.2 | async-start | bytes 262144
  146.3 158.9 %copy-start = (f32[512,1024]{1,0:T(8,128)S(1)}, f32[512,1024]{1,0:T(8,128)}, u32[]{:S(2)}) copy-start(f32[512,1024]{1,0:T(8,128)} %param.11) | copy-start | bytes 6291460
  1168.3 0.6 copy-start.2
Sparse Core Ops, SparseCore 0:
  9.0 49.1 all-gather.1
  63.1 69.2 all-reduce.3
  182.2 122.1 all-reduce.5
where the time goes:
time: 1180 us
  blocking collectives  480 us (41%)
  other arithmetic  328 us (28%)
  waiting for transfers between devices  174 us (15%)
  local copies, waits for them, and re-layouts  132 us (11%)
  matrix products  47.8 us (4%)
  between operations  13.3 us (1%)
    another operation x24, other arithmetic, advance(): jax.scipy.linalg.solve_triangular(column_part, whole_rest.T, lower=True)  322 us
    psum x8, blocking collectives, spread(): return lax.psum(kept, axis)  307 us
    psum x8, blocking collectives, advance(): whole_rest = lax.psum(remaining, 'gen')  133 us
    unnamed x4, waiting for transfers between devices  123 us
    another operation x96, local copies, waits for them, and re-layouts  80.2 us
    all_gather x1, waiting for transfers between devices, on_device(): orbital_side = lax.all_gather(collocation, 'fit', axis=1, tiled=True)  50.9 us
    psum x1, blocking collectives, on_device(): pivot_block = lax.psum(own_entries, ('gen', 'fit'))  39.1 us
    dot_general x8, matrix products, one_block(): jnp.einsum('apq,pn->aqn', vectors, pieces[0], preferred_element_type=jnp....  25.1 us
  transfers between devices with their start and end apart: 3, of which 2 were waited for; matrix products, arithmetic and copies ran while one was open for 4% of the time, Pallas kernels for 0%

commit v1 on v0

--- a/solution.py
+++ b/solution.py
@@ -60,7 +60,14 @@
     group_ratio = fit_count // gen_count
     owner_index = fit_index // group_ratio
     portion = fit_index % group_ratio
-    orbital_side = lax.all_gather(collocation, "fit", axis=1, tiled=True)
+    ways, here = (lax.axis_size("fit"), lax.axis_index("fit"))
+    orbital_side, reach = (collocation, 1)
+    while reach < ways:
+        theirs = lax.ppermute(orbital_side, "fit", [(d, d ^ reach) for d in range(ways)])
+        mine_first = jnp.concatenate([orbital_side, theirs], axis=1)
+        theirs_first = jnp.concatenate([theirs, orbital_side], axis=1)
+        orbital_side = jnp.where(here & reach == 0, mine_first, theirs_first)
+        reach = 2 * reach
     wide_slice = lax.dynamic_slice_in_dim(orbital_side, portion * pair_block, pair_block, 0)
     pair_side = spread(wide_slice, "gen", owner_index)
     partial_panel = project_block(

time: 1180 us -> 1260 us (1.068)
  waiting for transfers between devices: 174 us -> 237 us
    ppermute x0 -> x3, waiting for transfers between devices: none -> 114 us  [on_device(): lax.ppermute(orbital_side, 'fit', [(d, d ^ reach) for d in range(ways)])]
    all_gather x1 -> x0, waiting for transfers between devices: 50.9 us -> none  [on_device(): orbital_side = lax.all_gather(collocation, 'fit', axis=1, tiled=True)]
    unnamed x4 -> x3, waiting for transfers between devices: 123 us -> 123 us
  transfers between devices with their start and end apart: 3 -> 5, of which waited for: 2 -> 4; matrix products, arithmetic and copies ran while one was open for 4% -> 3% of each run, Pallas kernels for 0% -> 0%
where the time goes in v1:
time: 1260 us
  blocking collectives  481 us (38%)
  other arithmetic  339 us (27%)
  waiting for transfers between devices  237 us (19%)
  local copies, waits for them, and re-layouts  133 us (11%)
  matrix products  47.8 us (4%)
  between operations  13.6 us (1%)
    another operation x24, other arithmetic, advance(): jax.scipy.linalg.solve_triangular(column_part, whole_rest.T, lower=True)  322 us
    psum x8, blocking collectives, spread(): return lax.psum(kept, axis)  307 us
    psum x8, blocking collectives, advance(): whole_rest = lax.psum(remaining, 'gen')  133 us
    unnamed x3, waiting for transfers between devices  123 us
    ppermute x3, waiting for transfers between devices, on_device(): lax.ppermute(orbital_side, 'fit', [(d, d ^ reach) for d in range(ways)])  114 us
    another operation x96, local copies, waits for them, and re-layouts  80.2 us
    psum x1, blocking collectives, on_device(): pivot_block = lax.psum(own_entries, ('gen', 'fit'))  40.1 us
  transfers between devices with their start and end apart: 5, of which 4 were waited for; matrix products, arithmetic and copies ran while one was open for 3% of the time, Pallas kernels for 0%

profile of v1, /device:TPU:0, one launch (start us, length us, event | category | flops | bytes accessed | tf_op | source)
XLA Modules:
  0.0 1259.3 jit_solution(13052507777995914292)
XLA Ops:
  14.6 23.3 %collective-permute-done.1 = bf16[500,1024]{1,0:T(8,128)(2,1)S(1)} collective-permute-done((bf16[500,1024]{1,0:T(8,128)(2,1)}, bf16[500,1024]{1,0:T(8,128)(2,1)S(1)}, u32[]{:S(2)}, u32[]{:S(2)}) %collective-permute-start.1) | collective-permute-done | bytes 1024032 | tf_op jit(solution)/shard_map/ppermute | solution.py:66
  46.0 89.1 %collective-permute-done.2 = bf16[500,2048]{1,0:T(8,128)(2,1)} collective-permute-done((bf16[500,2048]{1,0:T(8,128)(2,1)}, bf16[500,2048]{1,0:T(8,128)(2,1)}, u32[]{:S(2)}, u32[]{:S(2)}) %collective-permute-start.2) | collective-permute-done | bytes 2048032 | tf_op jit(solution)/shard_map/ppermute | solution.py:66
  135.1 3.9 copy.29
  139.0 6.4 fusion.31
  149.3 40.1 %psum.42 = f32[8,8]{0,1:T(8,128)S(1)} all-reduce(f32[8,8]{0,1:T(8,128)S(1)} %bitcast.114), channel_id=1, replica_groups=mesh['gen'=4,'fit'=8] {'gen','fit'}, use_global_device_ids=true, to_apply=%region_2.3 | all-reduce | flops 64 | bytes 512 | tf_op jit(solution)/shard_map/psum | solution.py:55
  192.2 7.3 reshape.139
  199.5 4.0 reshape.113
  206.5 4.2 reshape.141
  210.8 6.0 reshape.114
  222.6 6.5 copy.37
  229.1 35.0 %while.31 = (s32[]{:T(128)}, f32[8,8,512]{2,1,0:T(8,128)S(1)}, bf16[8,500,512]{2,1,0:T(8,128)(2,1)}, bf16[8,500,250]{2,1,0:T(8,128)(2,1)}, bf16[8,250,512]{1,2,0:T(8,128)(2,1)}, /*index=5*/s32[]{:T(128)}) while((s32[]{:T(128)}, f32[8,8,512]{2,1,0:T(8,128)S(1)}, bf16[8,500,512]{2,1,0:T(8,128)(2,1)}, bf16[8,500,250]{2,1,0:T(8,128)(2,1)}, ...), condition=%wide.region_7.8_spmd, body=%wide.region_5.7_spmd.sunk | while | flops 1026171904 | bytes 4934221 | solution.py:33
  230.5 3.1 fusion.75
  239.2 3.1 fusion.75
  243.5 3.1 fusion.75
  265.0 123.0 %all-reduce.6.cloned.1.call-done = f32[64,512]{1,0:T(8,128)} async-done(((f32[64,512]{1,0:T(8,128)}), f32[64,512]{1,0:T(8,128)}) %all-reduce.6.cloned.1.call-update) | async-done | bytes 131088
  388.7 863.1 %while.33 = (s32[]{:T(128)}, f32[8,512]{1,0:T(8,128)S(1)}, f32[2,512]{1,0:T(2,128)S(1)}, s32[]{:T(128)}, s32[]{:T(128)}, /*index=5*/f32[512,1024]{1,0:T(8,128)S(...) while((s32[]{:T(128)}, f32[8,512]{1,0:T(8,128)S(1)}, ...), condition=%wide.region_12.13_spmd.clone, body=%wide.region_9.12_spmd.clone.sunk | while | flops 41468964 | bytes 4176043 | solution.py:101
  389.1 10.0 while.34
  399.2 40.1 %custom-call.26 = f32[4,128,128]{1,2,0:T(8,128)S(1)} custom-call(f32[4,128,128]{2,1,0:T(8,128)} %get-tuple-element.386), custom_call_target="InvertDiagBlocksLowerTriangular" | custom-call | tf_op jit(solution)/shard_map/while/body/eval_jaxpr/jit(_solve_triangular)/triangular_solve | solution.py:90
  439.3 15.9 %psum.48 = f32[512,8]{0,1:T(8,128)S(1)} all-reduce(f32[512,8]{0,1:T(8,128)S(1)} %bitcast.111), channel_id=1, replica_groups=mesh['gen'=4,'fit'=8] {'gen'}, use_global_device_ids=true, to_apply=%region_10.10 | all-reduce | flops 4096 | bytes 32768 | tf_op jit(solution)/shard_map/while/body/eval_jaxpr/psum | solution.py:88
  456.7 38.4 %psum.49 = f32[8,512]{1,0:T(8,128)S(1)} all-reduce(f32[8,512]{1,0:T(8,128)S(1)} %fusion.93), channel_id=1, replica_groups=mesh['gen'=4,'fit'=8] {'gen','fit'}, use_global_device_ids=true, to_apply=%region_11.11 | all-reduce | flops 4096 | bytes 32768 | tf_op jit(solution)/shard_map/while/body/eval_jaxpr/psum | solution.py:12
  496.3 10.0 while.34
  506.3 40.1 %custom-call.26 = f32[4,128,128]{1,2,0:T(8,128)S(1)} custom-call(f32[4,128,128]{2,1,0:T(8,128)} %get-tuple-element.386), custom_call_target="InvertDiagBlocksLowerTriangular" | custom-call | tf_op jit(solution)/shard_map/while/body/eval_jaxpr/jit(_solve_triangular)/triangular_solve | solution.py:90
  546.5 16.7 %psum.48 = f32[512,8]{0,1:T(8,128)S(1)} all-reduce(f32[512,8]{0,1:T(8,128)S(1)} %bitcast.111), channel_id=1, replica_groups=mesh['gen'=4,'fit'=8] {'gen'}, use_global_device_ids=true, to_apply=%region_10.10 | all-reduce | flops 4096 | bytes 32768 | tf_op jit(solution)/shard_map/while/body/eval_jaxpr/psum | solution.py:88
  564.7 38.4 %psum.49 = f32[8,512]{1,0:T(8,128)S(1)} all-reduce(f32[8,512]{1,0:T(8,128)S(1)} %fusion.93), channel_id=1, replica_groups=mesh['gen'=4,'fit'=8] {'gen','fit'}, use_global_device_ids=true, to_apply=%region_11.11 | all-reduce | flops 4096 | bytes 32768 | tf_op jit(solution)/shard_map/while/body/eval_jaxpr/psum | solution.py:12
  604.3 10.0 while.34
  614.3 40.1 %custom-call.26 = f32[4,128,128]{1,2,0:T(8,128)S(1)} custom-call(f32[4,128,128]{2,1,0:T(8,128)} %get-tuple-element.386), custom_call_target="InvertDiagBlocksLowerTriangular" | custom-call | tf_op jit(solution)/shard_map/while/body/eval_jaxpr/jit(_solve_triangular)/triangular_solve | solution.py:90
  654.4 16.7 %psum.48 = f32[512,8]{0,1:T(8,128)S(1)} all-reduce(f32[512,8]{0,1:T(8,128)S(1)} %bitcast.111), channel_id=1, replica_groups=mesh['gen'=4,'fit'=8] {'gen'}, use_global_device_ids=true, to_apply=%region_10.10 | all-reduce | flops 4096 | bytes 32768 | tf_op jit(solution)/shard_map/while/body/eval_jaxpr/psum | solution.py:88
  672.6 38.4 %psum.49 = f32[8,512]{1,0:T(8,128)S(1)} all-reduce(f32[8,512]{1,0:T(8,128)S(1)} %fusion.93), channel_id=1, replica_groups=mesh['gen'=4,'fit'=8] {'gen','fit'}, use_global_device_ids=true, to_apply=%region_11.11 | all-reduce | flops 4096 | bytes 32768 | tf_op jit(solution)/shard_map/while/body/eval_jaxpr/psum | solution.py:12
  712.2 10.0 while.34
  722.3 40.1 %custom-call.26 = f32[4,128,128]{1,2,0:T(8,128)S(1)} custom-call(f32[4,128,128]{2,1,0:T(8,128)} %get-tuple-element.386), custom_call_target="InvertDiagBlocksLowerTriangular" | custom-call | tf_op jit(solution)/shard_map/while/body/eval_jaxpr/jit(_solve_triangular)/triangular_solve | solution.py:90
  762.4 16.7 %psum.48 = f32[512,8]{0,1:T(8,128)S(1)} all-reduce(f32[512,8]{0,1:T(8,128)S(1)} %bitcast.111), channel_id=1, replica_groups=mesh['gen'=4,'fit'=8] {'gen'}, use_global_device_ids=true, to_apply=%region_10.10 | all-reduce | flops 4096 | bytes 32768 | tf_op jit(solution)/shard_map/while/body/eval_jaxpr/psum | solution.py:88
  780.6 38.4 %psum.49 = f32[8,512]{1,0:T(8,128)S(1)} all-reduce(f32[8,512]{1,0:T(8,128)S(1)} %fusion.93), channel_id=1, replica_groups=mesh['gen'=4,'fit'=8] {'gen','fit'}, use_global_device_ids=true, to_apply=%region_11.11 | all-reduce | flops 4096 | bytes 32768 | tf_op jit(solution)/shard_map/while/body/eval_jaxpr/psum | solution.py:12
  820.2 10.0 while.34
  830.2 40.1 %custom-call.26 = f32[4,128,128]{1,2,0:T(8,128)S(1)} custom-call(f32[4,128,128]{2,1,0:T(8,128)} %get-tuple-element.386), custom_call_target="InvertDiagBlocksLowerTriangular" | custom-call | tf_op jit(solution)/shard_map/while/body/eval_jaxpr/jit(_solve_triangular)/triangular_solve | solution.py:90
  870.3 16.7 %psum.48 = f32[512,8]{0,1:T(8,128)S(1)} all-reduce(f32[512,8]{0,1:T(8,128)S(1)} %bitcast.111), channel_id=1, replica_groups=mesh['gen'=4,'fit'=8] {'gen'}, use_global_device_ids=true, to_apply=%region_10.10 | all-reduce | flops 4096 | bytes 32768 | tf_op jit(solution)/shard_map/while/body/eval_jaxpr/psum | solution.py:88
  888.5 38.4 %psum.49 = f32[8,512]{1,0:T(8,128)S(1)} all-reduce(f32[8,512]{1,0:T(8,128)S(1)} %fusion.93), channel_id=1, replica_groups=mesh['gen'=4,'fit'=8] {'gen','fit'}, use_global_device_ids=true, to_apply=%region_11.11 | all-reduce | flops 4096 | bytes 32768 | tf_op jit(solution)/shard_map/while/body/eval_jaxpr/psum | solution.py:12
  928.1 10.0 while.34
  938.2 40.1 %custom-call.26 = f32[4,128,128]{1,2,0:T(8,128)S(1)} custom-call(f32[4,128,128]{2,1,0:T(8,128)} %get-tuple-element.386), custom_call_target="InvertDiagBlocksLowerTriangular" | custom-call | tf_op jit(solution)/shard_map/while/body/eval_jaxpr/jit(_solve_triangular)/triangular_solve | solution.py:90
  978.3 16.8 %psum.48 = f32[512,8]{0,1:T(8,128)S(1)} all-reduce(f32[512,8]{0,1:T(8,128)S(1)} %bitcast.111), channel_id=1, replica_groups=mesh['gen'=4,'fit'=8] {'gen'}, use_global_device_ids=true, to_apply=%region_10.10 | all-reduce | flops 4096 | bytes 32768 | tf_op jit(solution)/shard_map/while/body/eval_jaxpr/psum | solution.py:88
  996.5 38.4 %psum.49 = f32[8,512]{1,0:T(8,128)S(1)} all-reduce(f32[8,512]{1,0:T(8,128)S(1)} %fusion.93), channel_id=1, replica_groups=mesh['gen'=4,'fit'=8] {'gen','fit'}, use_global_device_ids=true, to_apply=%region_11.11 | all-reduce | flops 4096 | bytes 32768 | tf_op jit(solution)/shard_map/while/body/eval_jaxpr/psum | solution.py:12
  1036.1 10.0 while.34
  1046.1 40.1 %custom-call.26 = f32[4,128,128]{1,2,0:T(8,128)S(1)} custom-call(f32[4,128,128]{2,1,0:T(8,128)} %get-tuple-element.386), custom_call_target="InvertDiagBlocksLowerTriangular" | custom-call | tf_op jit(solution)/shard_map/while/body/eval_jaxpr/jit(_solve_triangular)/triangular_solve | solution.py:90
  1086.3 16.8 %psum.48 = f32[512,8]{0,1:T(8,128)S(1)} all-reduce(f32[512,8]{0,1:T(8,128)S(1)} %bitcast.111), channel_id=1, replica_groups=mesh['gen'=4,'fit'=8] {'gen'}, use_global_device_ids=true, to_apply=%region_10.10 | all-reduce | flops 4096 | bytes 32768 | tf_op jit(solution)/shard_map/while/body/eval_jaxpr/psum | solution.py:88
  1104.5 38.4 %psum.49 = f32[8,512]{1,0:T(8,128)S(1)} all-reduce(f32[8,512]{1,0:T(8,128)S(1)} %fusion.93), channel_id=1, replica_groups=mesh['gen'=4,'fit'=8] {'gen','fit'}, use_global_device_ids=true, to_apply=%region_11.11 | all-reduce | flops 4096 | bytes 32768 | tf_op jit(solution)/shard_map/while/body/eval_jaxpr/psum | solution.py:12
  1144.0 10.0 while.34
  1154.1 40.1 %custom-call.26 = f32[4,128,128]{1,2,0:T(8,128)S(1)} custom-call(f32[4,128,128]{2,1,0:T(8,128)} %get-tuple-element.386), custom_call_target="InvertDiagBlocksLowerTriangular" | custom-call | tf_op jit(solution)/shard_map/while/body/eval_jaxpr/jit(_solve_triangular)/triangular_solve | solution.py:90
  1194.2 16.8 %psum.48 = f32[512,8]{0,1:T(8,128)S(1)} all-reduce(f32[512,8]{0,1:T(8,128)S(1)} %bitcast.111), channel_id=1, replica_groups=mesh['gen'=4,'fit'=8] {'gen'}, use_global_device_ids=true, to_apply=%region_10.10 | all-reduce | flops 4096 | bytes 32768 | tf_op jit(solution)/shard_map/while/body/eval_jaxpr/psum | solution.py:88
  1212.4 38.4 %psum.49 = f32[8,512]{1,0:T(8,128)S(1)} all-reduce(f32[8,512]{1,0:T(8,128)S(1)} %fusion.93), channel_id=1, replica_groups=mesh['gen'=4,'fit'=8] {'gen','fit'}, use_global_device_ids=true, to_apply=%region_11.11 | all-reduce | flops 4096 | bytes 32768 | tf_op jit(solution)/shard_map/while/body/eval_jaxpr/psum | solution.py:12
  (301 shorter events, 159.7 us)
Async XLA Ops:
  6.5 222.6 %all-reduce.4.cloned.1.call-start = ((), (), s32[]{:S(2)}) async-start(), calls=%async_computation | async-start | bytes 4194304 | tf_op jit(solution)/shard_map/psum | solution.py:12
  7.8 30.2 %copy-start.4 = (bf16[500,512]{0,1:T(8,128)(2,1)}, bf16[500,512]{0,1:T(8,128)(2,1)S(1)}, u32[]{:S(2)}) copy-start(bf16[500,512]{0,1:T(8,128)(2,1)S(1)} %copy.20) | copy-start | bytes 1536004
  7.8 2.1 collective-permute-start
  9.9 28.1 %copy-start.5 = (bf16[500,512]{0,1:T(8,128)(2,1)}, bf16[500,512]{0,1:T(8,128)(2,1)S(1)}, u32[]{:S(2)}) copy-start(bf16[500,512]{0,1:T(8,128)(2,1)S(1)} %collective-permute-done) | copy-start | bytes 1536004
  10.3 4.4 copy-start.2
  11.7 26.3 %collective-permute-start.1 = (bf16[500,1024]{1,0:T(8,128)(2,1)}, bf16[500,1024]{1,0:T(8,128)(2,1)S(1)}, u32[]{:S(2)}, u32[]{:S(2)}) collective-permute-start(bf16[500,1024]{1,0:T(8,128)(2,1)} %copy.24), channel_id=1, source_target_pairs={{0,2},{1,3},{2,0},{3,1},{4,6},{5,7},{6,4},{7,5},{8,10},{9,11},{10,... | collective-permute-start | bytes 3072008 | tf_op jit(solution)/shard_map/ppermute | solution.py:66
  40.7 5.3 copy-start.7
  43.2 91.9 %collective-permute-start.2 = (bf16[500,2048]{1,0:T(8,128)(2,1)}, bf16[500,2048]{1,0:T(8,128)(2,1)}, u32[]{:S(2)}, u32[]{:S(2)}) collective-permute-start(bf16[500,2048]{1,0:T(8,128)(2,1)} %copy.28), channel_id=1, source_target_pairs={{0,4},{1,5},{2,6},{3,7},{4,0},{5,1},{6,2},{7,3},{8,12},{9,13},{10,... | collective-permute-start | bytes 6144008 | tf_op jit(solution)/shard_map/ppermute | solution.py:66
  145.4 1.6 copy-start.3
  145.5 242.5 %all-reduce.6.cloned.1.call-start = ((), (), s32[]{:S(2)}) async-start(), calls=%async_computation.1 | async-start | bytes 262144
  218.6 1.6 copy-start.1
  229.1 159.6 %copy-start = (f32[512,1024]{1,0:T(8,128)S(1)}, f32[512,1024]{1,0:T(8,128)}, u32[]{:S(2)}) copy-start(f32[512,1024]{1,0:T(8,128)} %param.11) | copy-start | bytes 6291460
  1251.8 0.6 copy-start.6
Sparse Core Ops, SparseCore 0:
  145.6 71.4 all-reduce.3
  265.1 122.8 all-reduce.5
